TPU v7x, 32 devices: a whole 2x2x4 slice. The times are simulated.
32 devices in a mesh: sec: 8 (over y, x, core), blk: 4 (over z).
Axes of the slice: x: 2, y: 2, z: 4, core: 2. Of those that a mesh axis runs over, the one named last changes fastest.
Arguments:
- two_site: bfloat16 [256, 768, 768], P('sec', 'blk'), may hold values from -6 to 6
- left_env: bfloat16 [8, 768, 768], P('sec', 'blk'), may hold values from -0.21875 to 0.21875
- right_env: bfloat16 [8, 768, 768], P('sec', 'blk'), may hold values from -0.21875 to 0.21875
- left_size: int32 [8], replicated, may hold values from 1 to 768, 4608 in all
- right_size: int32 [8], replicated, may hold values from 1 to 768, 4608 in all
Outputs:
- gram: float32 [8, 768, 768], P('sec', 'blk')
All inputs are finite; a program needn't handle non-finite values.
Results may differ from a plain program's by a relative error of at most 0.00096.
Values may be sent and summed in bfloat16 or wider, within the bound.
No kernel may reach another device: no remote copies, remote signals or barrier semaphores. Data moves between devices by JAX's collectives and lax.ppermute only.
A program may use at most 64 MiB of HBM per device.

v0:
```python
import functools
import jax
import jax.numpy as jnp
from jax import lax
from jax.experimental import pallas as pl
from jax.experimental.pallas import tpu as pltpu
from jax.sharding import PartitionSpec as P

STATES = 2
PAIRS = 16
PAD = 16
WINDOW = 3


def charge(level):
    return (level + 1) // 2


def rotate(block, axis, distance):
    size = lax.axis_size(axis)
    return lax.ppermute(block, axis, [(i, (i + distance) % size) for i in range(size)])


def pick_value(table, position):
    hits = jnp.arange(table.shape[0], dtype=jnp.int32) == position
    return jnp.sum(jnp.where(hits, table, jnp.zeros_like(table)))


def live_rows(block, live, first_row):
    rows, width = block.shape
    row_ids = first_row + jnp.arange(rows, dtype=jnp.int32)
    column_ids = jnp.arange(width, dtype=jnp.int32)
    keep = (row_ids[:, None] < live) & (column_ids[None, :] < live)
    return jnp.where(keep, block, jnp.zeros_like(block))


def block_kernel(groups, first, last, scale, where_ref, *refs):
    left_ref, right_ref = refs[:2]
    pieces = refs[2 : 2 + groups]
    rest = refs[2 + groups :]
    if not first:
        before_ref, rest = rest[0], rest[1:]
    if last:
        sends, (total_ref, block_ref) = rest[:groups], rest[groups:]
    else:
        total_ref, block_ref = rest
    rows = pieces[0].shape[-2]
    z = where_ref[0]
    for s in range(groups):
        start = pl.multiple_of(lax.rem(z + groups - s, groups) * rows, rows)
        block_ref[pl.ds(start, rows), :] = pieces[s][0]
    half = jnp.dot(
        left_ref[...], block_ref[...], preferred_element_type=jnp.float32
    ).astype(jnp.bfloat16)
    applied = lax.dot_general(
        right_ref[...], half, (((1,), (1,)), ((), ())), preferred_element_type=jnp.float32
    ).astype(jnp.bfloat16)
    square = lax.dot_general(
        applied, applied, (((1,), (1,)), ((), ())), preferred_element_type=jnp.float32
    )
    if first:
        total_ref[...] = square
    else:
        total_ref[...] = before_ref[...] + square
    if last:
        width = total_ref.shape[1]
        for s in range(groups):
            start = pl.multiple_of(lax.rem(z + s, groups) * rows, rows)
            part = scale * total_ref[pl.ds(start, rows), :]
            short = part.astype(jnp.bfloat16)
            row_ids = start + lax.broadcasted_iota(jnp.int32, (rows, width), 0)
            column_ids = lax.broadcasted_iota(jnp.int32, (rows, width), 1)
            gap = jnp.where(row_ids == column_ids, part - short.astype(jnp.float32), 0.0)
            gap = jnp.sum(gap, axis=0, keepdims=True)
            sends[s][:rows, :] = short
            sends[s][rows:, :] = jnp.broadcast_to(gap, (PAD, width)).astype(jnp.bfloat16)


def one_block(z, left, right, two_site, own_base, pieces, before, last, scale):
    groups = len(pieces) + 1
    rows, width = pieces[0].shape
    first = before is None
    whole = pl.BlockSpec((width, width), lambda i, w: (0, 0))
    piece_spec = pl.BlockSpec((1, rows, width), lambda i, w: (0, 0, 0))
    own_spec = pl.BlockSpec((1, rows, width), lambda i, w: (w[1], 0, 0))
    in_specs = [whole, whole, own_spec] + [piece_spec] * (groups - 1)
    operands = [left, right, two_site] + [p[None] for p in pieces]
    if not first:
        in_specs.append(whole)
        operands.append(before)
    scratch = [pltpu.VMEM((width, width), jnp.bfloat16)]
    if last:
        out_shape = [jax.ShapeDtypeStruct((rows + PAD, width), jnp.bfloat16)] * groups
        out_specs = [pl.BlockSpec((rows + PAD, width), lambda i, w: (0, 0))] * groups
        scratch = [pltpu.VMEM((width, width), jnp.float32)] + scratch
        aliases = {}
    else:
        out_shape = jax.ShapeDtypeStruct((width, width), jnp.float32)
        out_specs = whole
        aliases = {} if first else {len(operands): 0}
    return pl.pallas_call(
        functools.partial(block_kernel, groups, first, last, scale),
        out_shape=out_shape,
        grid_spec=pltpu.PrefetchScalarGridSpec(
            num_scalar_prefetch=1, grid=(1,), in_specs=in_specs, out_specs=out_specs,
            scratch_shapes=scratch,
        ),
        input_output_aliases=aliases,
        cost_estimate=pl.CostEstimate(
            flops=6 * width**3, transcendentals=0, bytes_accessed=12 * width * width
        ),
        name="last_block" if last else "one_block",
    )(jnp.stack([z, own_base]), *operands)


def named(block, distance):
    if not distance:
        return block
    return rotate(block, "blk", distance)


def body(two_site, left_env, right_env, left_size, right_size):
    sectors = lax.axis_size("sec")
    groups = lax.axis_size("blk")
    sec_index = lax.axis_index("sec")
    blk_index = lax.axis_index("blk")
    total_blocks, rows, width = two_site.shape
    pairs_here = PAIRS // groups
    here = total_blocks // groups
    behind = [(blk_index - s) % groups for s in range(groups)]
    ahead = [(blk_index + s) % groups for s in range(groups)]

    left_own = live_rows(left_env[0], pick_value(left_size, sec_index), blk_index * rows)
    left_parts = [named(left_own, s) for s in range(groups)]
    right_own = live_rows(right_env[0], pick_value(right_size, sec_index), blk_index * rows)
    right_parts = [named(right_own, s) for s in range(groups)]
    left_full = jnp.concatenate(left_parts, axis=0)
    right_full = jnp.take(jnp.stack(right_parts), jnp.stack(behind), axis=0)
    right_full = right_full.reshape(width, width)

    right_of = []
    arrived = {}
    for j in range(pairs_here):
        route = []
        for b in range(sectors):
            for z in range(groups):
                pair = z * pairs_here + j
                step = charge(pair // 4) + charge(pair % 4)
                route.append((b * groups + z, (b - step) % sectors * groups + z))
        key = tuple(route)
        if key not in arrived:
            arrived[key] = lax.ppermute(right_full, ("sec", "blk"), route)
        right_of.append(arrived[key])

    totals = []
    for c in range(here):
        pieces = [
            lax.dynamic_index_in_dim(two_site, ahead[s] * here + c, 0, keepdims=False)
            for s in range(1, groups)
        ]
        if c >= WINDOW:
            pieces, totals[c - WINDOW] = lax.optimization_barrier((pieces, totals[c - WINDOW]))
        pieces = [named(p, s + 1) for s, p in enumerate(pieces)]
        totals.append(
            one_block(
                blk_index, left_full, right_of[c // STATES], two_site, blk_index * here + c,
                pieces, totals[-1] if c else None, c == here - 1, 1.0 / (8.0 * width),
            )
        )
    total = totals[-1]

    gram_rows = jnp.zeros((rows, width), jnp.float32)
    row_ids = blk_index * rows + jnp.arange(rows, dtype=jnp.int32)
    on_diagonal = row_ids[:, None] == jnp.arange(width, dtype=jnp.int32)[None, :]
    for s in range(groups):
        route = []
        for b in range(sectors):
            for z in range(groups):
                up = charge(z * pairs_here // 4)
                route.append((b * groups + z, (b + up) % sectors * groups + (z + s) % groups))
        part = lax.ppermute(total[s], ("sec", "blk"), route).astype(jnp.float32)
        gram_rows = gram_rows + part[:rows] + jnp.where(on_diagonal, part[rows][None, :], 0.0)
    return gram_rows[None]


def solution(mesh):
    placed = (P("sec", "blk", None), P("sec", "blk", None), P("sec", "blk", None), P(), P())
    return jax.shard_map(
        body, mesh=mesh, in_specs=placed, out_specs=P("sec", "blk", None), check_vma=False
    )
```

profile of v0, /device:TPU:0, one launch (start us, length us, event | category | flops | bytes accessed | tf_op | source)
XLA Modules:
  0.0 303.8 jit_solution(17720978597110051216)
XLA Ops:
  3.6 5.1 %collective-permute-start.5 = (bf16[192,768]{1,0:T(8,128)(2,1)S(1)}, bf16[192,768]{1,0:T(8,128)(2,1)S(1)}, u32[]{:S(2)}, u32[]{:S(2)}) collective-permute-start(bf16[192,768]{1,0:T(8,128)(2,1)S(1)} %and_select_fusion), channel_id=1, source_target_pairs={{0,3},{1,0},{2,1},{3,2},{4,7},{5,4},{6,5},{7,6},{8,11},{9,8},{10,9... | collective-permute-start | bytes 884744 | tf_op jit(solution)/shard_map/ppermute | solution.py:21
  9.7 4.7 %dynamic-slice_bitcast_fusion = (bf16[192,768]{1,0:T(8,128)(2,1)}, bf16[192,768]{1,0:T(8,128)(2,1)}, bf16[192,768]{1,0:T(8,128)(2,1)}, bf16[192,768]{1,0:T(8,128...) fusion(bf16[32,192,768]{2,1,0:T(8,128)(2,1)} %refs_2_.15, ...), kind=kLoop, calls=%fused_computation.16 | loop fusion | bytes 10616904 | tf_op jit(solution)/shard_map/jit(dynamic_index_in_dim)/squeeze | solution.py:158
  14.4 3.4 %collective-permute-start.12 = (bf16[192,768]{1,0:T(8,128)(2,1)}, bf16[192,768]{1,0:T(8,128)(2,1)}, u32[]{:S(2)}, u32[]{:S(2)}) collective-permute-start(bf16[192,768]{1,0:T(8,128)(2,1)} %get-tuple-element.57), channel_id=1, source_target_pairs={{0,1},{1,2},{2,3},{3,0},{4,5},{5,6},{6,7},{7,4},{8,9},{9,10},{10,1... | collective-permute-start | bytes 884744 | tf_op jit(solution)/shard_map/ppermute | solution.py:21
  23.4 24.3 %collective-permute-done.4 = bf16[192,768]{1,0:T(8,128)(2,1)S(1)} collective-permute-done((bf16[192,768]{1,0:T(8,128)(2,1)S(1)}, bf16[192,768]{1,0:T(8,128)(2,1)S(1)}, u32[]{:S(2)}, u32[]{:S(2)}) %collective-permute-start.4) | collective-permute-done | bytes 294944 | tf_op jit(solution)/shard_map/ppermute | solution.py:21
  52.6 3.5 %collective-permute-start.1 = (bf16[192,768]{1,0:T(8,128)(2,1)S(1)}, bf16[192,768]{1,0:T(8,128)(2,1)}, u32[]{:S(2)}, u32[]{:S(2)}) collective-permute-start(bf16[192,768]{1,0:T(8,128)(2,1)S(1)} %and_select_fusion.2), channel_id=1, source_target_pairs={{0,2},{1,3},{2,0},{3,1},{4,6},{5,7},{6,4},{7,5},{8,10},{9,11},{10,... | collective-permute-start | bytes 884744 | tf_op jit(solution)/shard_map/ppermute | solution.py:21
  57.4 15.4 %collective-permute-start.2 = (bf16[192,768]{1,0:T(8,128)(2,1)S(1)}, bf16[192,768]{1,0:T(8,128)(2,1)}, u32[]{:S(2)}, u32[]{:S(2)}) collective-permute-start(bf16[192,768]{1,0:T(8,128)(2,1)S(1)} %and_select_fusion.2), channel_id=1, source_target_pairs={{0,3},{1,0},{2,1},{3,2},{4,7},{5,4},{6,5},{7,6},{8,11},{9,8},{10,9... | collective-permute-start | bytes 884744 | tf_op jit(solution)/shard_map/ppermute | solution.py:21
  73.4 3.6 %collective-permute-start.9 = (bf16[192,768]{1,0:T(8,128)(2,1)S(1)}, bf16[192,768]{1,0:T(8,128)(2,1)S(1)}, u32[]{:S(2)}, u32[]{:S(2)}) collective-permute-start(bf16[192,768]{1,0:T(8,128)(2,1)S(1)} %get-tuple-element.60), channel_id=1, source_target_pairs={{0,1},{1,2},{2,3},{3,0},{4,5},{5,6},{6,7},{7,4},{8,9},{9,10},{10,1... | collective-permute-start | bytes 884744 | tf_op jit(solution)/shard_map/ppermute | solution.py:21
  77.0 8.7 %collective-permute-done.1 = bf16[192,768]{1,0:T(8,128)(2,1)} collective-permute-done((bf16[192,768]{1,0:T(8,128)(2,1)S(1)}, bf16[192,768]{1,0:T(8,128)(2,1)}, u32[]{:S(2)}, u32[]{:S(2)}) %collective-permute-start.1) | collective-permute-done | bytes 294944 | tf_op jit(solution)/shard_map/ppermute | solution.py:21
  87.0 12.3 %collective-permute-start.11 = (bf16[192,768]{1,0:T(8,128)(2,1)}, bf16[192,768]{1,0:T(8,128)(2,1)S(1)}, u32[]{:S(2)}, u32[]{:S(2)}) collective-permute-start(bf16[192,768]{1,0:T(8,128)(2,1)} %get-tuple-element.58), channel_id=1, source_target_pairs={{0,3},{1,0},{2,1},{3,2},{4,7},{5,4},{6,5},{7,6},{8,11},{9,8},{10,9... | collective-permute-start | bytes 884744 | tf_op jit(solution)/shard_map/ppermute | solution.py:21
  102.6 8.4 %collective-permute-done.10 = bf16[192,768]{1,0:T(8,128)(2,1)} collective-permute-done((bf16[192,768]{1,0:T(8,128)(2,1)S(1)}, bf16[192,768]{1,0:T(8,128)(2,1)}, u32[]{:S(2)}, u32[]{:S(2)}) %collective-permute-start.10) | collective-permute-done | bytes 294944 | tf_op jit(solution)/shard_map/ppermute | solution.py:21
  116.5 2.9 collective-permute-start.23
  119.4 7.2 %one_block.7.refs_6_ = f32[768,768]{1,0:T(8,128)} custom-call(s32[2]{0:T(128)} %pad_add_fusion.3.where_ref, bf16[768,768]{1,0:T(8,128)(2,1)} %pad_maximum_fusion.refs_0_, bf16[768,768]{1,0:T(8,128)(2,1)} %copy-done.2, bf16[32,192,768]{2,1,0:T(8,128)(2,1)} %refs_2_.15, bf16[1,192,768]{2,1,0:T(8,128)(2,1)} %bitcast.33.refs_3_, ...), custom_call_target="tpu_custom_call" | custom-call | flops 2717908992 | bytes 7077888 | tf_op jit(solution)/shard_map/one_block/pallas_call | solution.py:101
  127.3 6.6 %collective-permute-done.22 = bf16[192,768]{1,0:T(8,128)(2,1)} collective-permute-done((bf16[192,768]{1,0:T(8,128)(2,1)}, bf16[192,768]{1,0:T(8,128)(2,1)}, u32[]{:S(2)}, u32[]{:S(2)}) %collective-permute-start.22) | collective-permute-done | bytes 294944 | tf_op jit(solution)/shard_map/ppermute | solution.py:21
  133.9 6.9 %collective-permute-start.20 = (bf16[192,768]{1,0:T(8,128)(2,1)}, bf16[192,768]{1,0:T(8,128)(2,1)}, u32[]{:S(2)}, u32[]{:S(2)}) collective-permute-start(bf16[192,768]{1,0:T(8,128)(2,1)} %get-tuple-element.29), channel_id=1, source_target_pairs={{0,3},{1,0},{2,1},{3,2},{4,7},{5,4},{6,5},{7,6},{8,11},{9,8},{10,9... | collective-permute-start | bytes 884744 | tf_op jit(solution)/shard_map/ppermute | solution.py:21
  140.8 8.1 %one_block.8.refs_6_ = f32[768,768]{1,0:T(8,128)} custom-call(s32[2]{0:T(128)} %pad_add_fusion.2.where_ref, bf16[768,768]{1,0:T(8,128)(2,1)} %pad_maximum_fusion.refs_0_, bf16[768,768]{1,0:T(8,128)(2,1)} %copy-done.2, bf16[32,192,768]{2,1,0:T(8,128)(2,1)} %refs_2_.15, bf16[1,192,768]{2,1,0:T(8,128)(2,1)} %bitcast.105, ...), custom_call_target="tpu_custom_call", output_to_operand_aliasing={{}: (7, {})} | custom-call | flops 2717908992 | bytes 7077888 | tf_op jit(solution)/shard_map/one_block/pallas_call | solution.py:101
  148.9 10.6 %collective-permute-start.15 = (bf16[192,768]{1,0:T(8,128)(2,1)S(1)}, bf16[192,768]{1,0:T(8,128)(2,1)}, u32[]{:S(2)}, u32[]{:S(2)}) collective-permute-start(bf16[192,768]{1,0:T(8,128)(2,1)S(1)} %copy-done.10), channel_id=1, source_target_pairs={{0,1},{1,2},{2,3},{3,0},{4,5},{5,6},{6,7},{7,4},{8,9},{9,10},{10,1... | collective-permute-start | bytes 884744 | tf_op jit(solution)/shard_map/ppermute | solution.py:21
  161.1 8.1 %one_block.9.refs_6_ = f32[768,768]{1,0:T(8,128)} custom-call(s32[2]{0:T(128)} %pad_add_fusion.5.where_ref, bf16[768,768]{1,0:T(8,128)(2,1)} %pad_maximum_fusion.refs_0_, bf16[768,768]{1,0:T(8,128)(2,1)} %copy-done, bf16[32,192,768]{2,1,0:T(8,128)(2,1)} %refs_2_.15, bf16[1,192,768]{2,1,0:T(8,128)(2,1)} %bitcast.50.refs_3_, ...), custom_call_target="tpu_custom_call", output_to_operand_aliasing={{}: (7, {})} | custom-call | flops 2717908992 | bytes 7077888 | tf_op jit(solution)/shard_map/one_block/pallas_call | solution.py:101
  172.1 14.0 %collective-permute-start.30 = (bf16[192,768]{1,0:T(8,128)(2,1)}, bf16[192,768]{1,0:T(8,128)(2,1)S(1)}, u32[]{:S(2)}, u32[]{:S(2)}) collective-permute-start(bf16[192,768]{1,0:T(8,128)(2,1)} %get-tuple-element.36), channel_id=1, source_target_pairs={{0,1},{1,2},{2,3},{3,0},{4,5},{5,6},{6,7},{7,4},{8,9},{9,10},{10,1... | collective-permute-start | bytes 884744 | tf_op jit(solution)/shard_map/ppermute | solution.py:21
  186.1 8.1 %one_block.10.refs_6_ = f32[768,768]{1,0:T(8,128)} custom-call(s32[2]{0:T(128)} %pad_add_fusion.4.where_ref, bf16[768,768]{1,0:T(8,128)(2,1)} %pad_maximum_fusion.refs_0_, bf16[768,768]{1,0:T(8,128)(2,1)} %copy-done, bf16[32,192,768]{2,1,0:T(8,128)(2,1)} %refs_2_.15, bf16[1,192,768]{2,1,0:T(8,128)(2,1)} %bitcast.108, ...), custom_call_target="tpu_custom_call", output_to_operand_aliasing={{}: (7, {})} | custom-call | flops 2717908992 | bytes 7077888 | tf_op jit(solution)/shard_map/one_block/pallas_call | solution.py:101
  197.3 9.7 %collective-permute-start.28 = (bf16[192,768]{1,0:T(8,128)(2,1)S(1)}, bf16[192,768]{1,0:T(8,128)(2,1)S(1)}, u32[]{:S(2)}, u32[]{:S(2)}) collective-permute-start(bf16[192,768]{1,0:T(8,128)(2,1)S(1)} %copy-done.12), channel_id=1, source_target_pairs={{0,2},{1,3},{2,0},{3,1},{4,6},{5,7},{6,4},{7,5},{8,10},{9,11},{10,... | collective-permute-start | bytes 884744 | tf_op jit(solution)/shard_map/ppermute | solution.py:21
  207.0 3.6 %collective-permute-start.29 = (bf16[192,768]{1,0:T(8,128)(2,1)S(1)}, bf16[192,768]{1,0:T(8,128)(2,1)}, u32[]{:S(2)}, u32[]{:S(2)}) collective-permute-start(bf16[192,768]{1,0:T(8,128)(2,1)S(1)} %copy-done.11), channel_id=1, source_target_pairs={{0,3},{1,0},{2,1},{3,2},{4,7},{5,4},{6,5},{7,6},{8,11},{9,8},{10,9... | collective-permute-start | bytes 884744 | tf_op jit(solution)/shard_map/ppermute | solution.py:21
  210.6 8.1 %one_block.11.refs_6_ = f32[768,768]{1,0:T(8,128)} custom-call(s32[2]{0:T(128)} %pad_add_fusion.1.where_ref, bf16[768,768]{1,0:T(8,128)(2,1)} %pad_maximum_fusion.refs_0_, bf16[768,768]{1,0:T(8,128)(2,1)} %copy-done, bf16[32,192,768]{2,1,0:T(8,128)(2,1)} %refs_2_.15, bf16[1,192,768]{2,1,0:T(8,128)(2,1)} %bitcast.38.refs_3_, ...), custom_call_target="tpu_custom_call", output_to_operand_aliasing={{}: (7, {})} | custom-call | flops 2717908992 | bytes 7077888 | tf_op jit(solution)/shard_map/one_block/pallas_call | solution.py:101
  220.3 4.0 %collective-permute-start.24 = (bf16[192,768]{1,0:T(8,128)(2,1)S(1)}, bf16[192,768]{1,0:T(8,128)(2,1)S(1)}, u32[]{:S(2)}, u32[]{:S(2)}) collective-permute-start(bf16[192,768]{1,0:T(8,128)(2,1)S(1)} %copy-done.7), channel_id=1, source_target_pairs={{0,1},{1,2},{2,3},{3,0},{4,5},{5,6},{6,7},{7,4},{8,9},{9,10},{10,1... | collective-permute-start | bytes 884744 | tf_op jit(solution)/shard_map/ppermute | solution.py:21
  224.3 3.4 %collective-permute-start.25 = (bf16[192,768]{1,0:T(8,128)(2,1)S(1)}, bf16[192,768]{1,0:T(8,128)(2,1)S(1)}, u32[]{:S(2)}, u32[]{:S(2)}) collective-permute-start(bf16[192,768]{1,0:T(8,128)(2,1)S(1)} %copy-done.6), channel_id=1, source_target_pairs={{0,2},{1,3},{2,0},{3,1},{4,6},{5,7},{6,4},{7,5},{8,10},{9,11},{10,... | collective-permute-start | bytes 884744 | tf_op jit(solution)/shard_map/ppermute | solution.py:21
  229.6 7.9 %one_block.12.refs_6_ = f32[768,768]{1,0:T(8,128)} custom-call(s32[2]{0:T(128)} %pad_add_fusion.7.where_ref, bf16[768,768]{1,0:T(8,128)(2,1)} %pad_maximum_fusion.refs_0_, bf16[768,768]{1,0:T(8,128)(2,1)} %copy-done, bf16[32,192,768]{2,1,0:T(8,128)(2,1)} %refs_2_.15, bf16[1,192,768]{2,1,0:T(8,128)(2,1)} %bitcast.107, ...), custom_call_target="tpu_custom_call", output_to_operand_aliasing={{}: (7, {})} | custom-call | flops 2717908992 | bytes 7077888 | tf_op jit(solution)/shard_map/one_block/pallas_call | solution.py:101
  237.6 8.0 %collective-permute-done.28 = bf16[192,768]{1,0:T(8,128)(2,1)S(1)} collective-permute-done((bf16[192,768]{1,0:T(8,128)(2,1)S(1)}, bf16[192,768]{1,0:T(8,128)(2,1)S(1)}, u32[]{:S(2)}, u32[]{:S(2)}) %collective-permute-start.28) | collective-permute-done | bytes 294944 | tf_op jit(solution)/shard_map/ppermute | solution.py:21
  246.3 7.9 %one_block.13.refs_6_ = f32[768,768]{1,0:T(8,128)} custom-call(s32[2]{0:T(128)} %pad_add_fusion.6.where_ref, bf16[768,768]{1,0:T(8,128)(2,1)} %pad_maximum_fusion.refs_0_, bf16[768,768]{1,0:T(8,128)(2,1)} %copy-done.1, bf16[32,192,768]{2,1,0:T(8,128)(2,1)} %refs_2_.15, bf16[1,192,768]{2,1,0:T(8,128)(2,1)} %bitcast.109, ...), custom_call_target="tpu_custom_call", output_to_operand_aliasing={{}: (7, {})} | custom-call | flops 2717908992 | bytes 7077888 | tf_op jit(solution)/shard_map/one_block/pallas_call | solution.py:101
  254.2 3.9 %collective-permute-done.25 = bf16[192,768]{1,0:T(8,128)(2,1)S(1)} collective-permute-done((bf16[192,768]{1,0:T(8,128)(2,1)S(1)}, bf16[192,768]{1,0:T(8,128)(2,1)S(1)}, u32[]{:S(2)}, u32[]{:S(2)}) %collective-permute-start.25) | collective-permute-done | bytes 294944 | tf_op jit(solution)/shard_map/ppermute | solution.py:21
  259.0 8.0 %last_block.1 = (bf16[208,768]{1,0:T(8,128)(2,1)}, bf16[208,768]{1,0:T(8,128)(2,1)}, bf16[208,768]{1,0:T(8,128)(2,1)}, bf16[208,768]{1,0:T(8,128)(2,1)}) custom-call(s32[2]{0:T(128)} %pad_add_fusion.where_ref, bf16[768,768]{1,0:T(8,128)(2,1)} %pad_maximum_fusion.refs_0_, bf16[768,768]{1,0:T(8,128)(2,1)} %copy-done.1, bf16[32,192,768]{2,1,0:T(8,128)(2,1)} %refs_2_.15, ...), custom_call_target="tpu_custom_call" | custom-call | flops 2717908992 | bytes 7077888 | tf_op jit(solution)/shard_map/last_block/pallas_call | solution.py:101
  267.0 6.6 %collective-permute-start.36 = (bf16[208,768]{1,0:T(8,128)(2,1)}, bf16[208,768]{1,0:T(8,128)(2,1)S(1)}, u32[]{:S(2)}, u32[]{:S(2)}) collective-permute-start(bf16[208,768]{1,0:T(8,128)(2,1)} %get-tuple-element.42), channel_id=1, source_target_pairs={{0,3},{1,4},{2,5},{3,10},{4,7},{5,8},{6,9},{7,14},{8,11},{9,12},{1... | collective-permute-start | bytes 958472 | tf_op jit(solution)/shard_map/ppermute | solution.py:181
  275.3 6.6 %collective-permute-done.36 = bf16[208,768]{1,0:T(8,128)(2,1)S(1)} collective-permute-done((bf16[208,768]{1,0:T(8,128)(2,1)}, bf16[208,768]{1,0:T(8,128)(2,1)S(1)}, u32[]{:S(2)}, u32[]{:S(2)}) %collective-permute-start.36) | collective-permute-done | bytes 319520 | tf_op jit(solution)/shard_map/ppermute | solution.py:181
  281.9 20.5 %collective-permute-done.35 = bf16[208,768]{1,0:T(8,128)(2,1)S(1)} collective-permute-done((bf16[208,768]{1,0:T(8,128)(2,1)}, bf16[208,768]{1,0:T(8,128)(2,1)S(1)}, u32[]{:S(2)}, u32[]{:S(2)}) %collective-permute-start.35) | collective-permute-done | bytes 319520 | tf_op jit(solution)/shard_map/ppermute | solution.py:181
  (137 shorter events, 43.5 us)
Async XLA Ops:
  8.7 39.0 %collective-permute-start.4 = (bf16[192,768]{1,0:T(8,128)(2,1)S(1)}, bf16[192,768]{1,0:T(8,128)(2,1)S(1)}, u32[]{:S(2)}, u32[]{:S(2)}) collective-permute-start(bf16[192,768]{1,0:T(8,128)(2,1)S(1)} %and_select_fusion), channel_id=1, source_target_pairs={{0,2},{1,3},{2,0},{3,1},{4,6},{5,7},{6,4},{7,5},{8,10},{9,11},{10,... | collective-permute-start | bytes 884744 | tf_op jit(solution)/shard_map/ppermute | solution.py:21
  14.4 38.2 %collective-permute-start.12 = (bf16[192,768]{1,0:T(8,128)(2,1)}, bf16[192,768]{1,0:T(8,128)(2,1)}, u32[]{:S(2)}, u32[]{:S(2)}) collective-permute-start(bf16[192,768]{1,0:T(8,128)(2,1)} %get-tuple-element.57), channel_id=1, source_target_pairs={{0,1},{1,2},{2,3},{3,0},{4,5},{5,6},{6,7},{7,4},{8,9},{9,10},{10,1... | collective-permute-start | bytes 884744 | tf_op jit(solution)/shard_map/ppermute | solution.py:21
  17.8 39.6 %collective-permute-start.13 = (bf16[192,768]{1,0:T(8,128)(2,1)}, bf16[192,768]{1,0:T(8,128)(2,1)}, u32[]{:S(2)}, u32[]{:S(2)}) collective-permute-start(bf16[192,768]{1,0:T(8,128)(2,1)} %get-tuple-element.56), channel_id=1, source_target_pairs={{0,2},{1,3},{2,0},{3,1},{4,6},{5,7},{6,4},{7,5},{8,10},{9,11},{10,... | collective-permute-start | bytes 884744 | tf_op jit(solution)/shard_map/ppermute | solution.py:21
  19.7 53.1 %collective-permute-start.14 = (bf16[192,768]{1,0:T(8,128)(2,1)S(1)}, bf16[192,768]{1,0:T(8,128)(2,1)}, u32[]{:S(2)}, u32[]{:S(2)}) collective-permute-start(bf16[192,768]{1,0:T(8,128)(2,1)S(1)} %get-tuple-element.55), channel_id=1, source_target_pairs={{0,3},{1,0},{2,1},{3,2},{4,7},{5,4},{6,5},{7,6},{8,11},{9,8},{10,9... | collective-permute-start | bytes 884744 | tf_op jit(solution)/shard_map/ppermute | solution.py:21
  49.7 66.4 %collective-permute-start.8 = (bf16[768,768]{1,0:T(8,128)(2,1)}, bf16[768,768]{1,0:T(8,128)(2,1)S(1)}, u32[]{:S(2)}, u32[]{:S(2)}) collective-permute-start(bf16[768,768]{1,0:T(8,128)(2,1)} %bitcast_select_fusion), channel_id=1, source_target_pairs={{0,0},{1,29},{2,30},{3,27},{4,4},{5,1},{6,2},{7,31},{8,8},{9,5},{1... | collective-permute-start | bytes 3538952 | tf_op jit(solution)/shard_map/ppermute | solution.py:152
  51.8 21.6 %collective-permute-start = (bf16[192,768]{1,0:T(8,128)(2,1)S(1)}, bf16[192,768]{1,0:T(8,128)(2,1)}, u32[]{:S(2)}, u32[]{:S(2)}) collective-permute-start(bf16[192,768]{1,0:T(8,128)(2,1)S(1)} %and_select_fusion.2), channel_id=1, source_target_pairs={{0,1},{1,2},{2,3},{3,0},{4,5},{5,6},{6,7},{7,4},{8,9},{9,10},{10,1... | collective-permute-start | bytes 884744 | tf_op jit(solution)/shard_map/ppermute | solution.py:21
  52.6 33.1 %collective-permute-start.1 = (bf16[192,768]{1,0:T(8,128)(2,1)S(1)}, bf16[192,768]{1,0:T(8,128)(2,1)}, u32[]{:S(2)}, u32[]{:S(2)}) collective-permute-start(bf16[192,768]{1,0:T(8,128)(2,1)S(1)} %and_select_fusion.2), channel_id=1, source_target_pairs={{0,2},{1,3},{2,0},{3,1},{4,6},{5,7},{6,4},{7,5},{8,10},{9,11},{10,... | collective-permute-start | bytes 884744 | tf_op jit(solution)/shard_map/ppermute | solution.py:21
  57.4 29.6 %collective-permute-start.2 = (bf16[192,768]{1,0:T(8,128)(2,1)S(1)}, bf16[192,768]{1,0:T(8,128)(2,1)}, u32[]{:S(2)}, u32[]{:S(2)}) collective-permute-start(bf16[192,768]{1,0:T(8,128)(2,1)S(1)} %and_select_fusion.2), channel_id=1, source_target_pairs={{0,3},{1,0},{2,1},{3,2},{4,7},{5,4},{6,5},{7,6},{8,11},{9,8},{10,9... | collective-permute-start | bytes 884744 | tf_op jit(solution)/shard_map/ppermute | solution.py:21
  72.8 76.1 %collective-permute-start.7 = (bf16[768,768]{1,0:T(8,128)(2,1)}, bf16[768,768]{1,0:T(8,128)(2,1)S(1)}, u32[]{:S(2)}, u32[]{:S(2)}) collective-permute-start(bf16[768,768]{1,0:T(8,128)(2,1)} %bitcast_select_fusion), channel_id=1, source_target_pairs={{0,28},{1,25},{2,26},{3,23},{4,0},{5,29},{6,30},{7,27},{8,4},{9,1}... | collective-permute-start | bytes 3538952 | tf_op jit(solution)/shard_map/ppermute | solution.py:152
  73.4 28.5 %collective-permute-start.9 = (bf16[192,768]{1,0:T(8,128)(2,1)S(1)}, bf16[192,768]{1,0:T(8,128)(2,1)S(1)}, u32[]{:S(2)}, u32[]{:S(2)}) collective-permute-start(bf16[192,768]{1,0:T(8,128)(2,1)S(1)} %get-tuple-element.60), channel_id=1, source_target_pairs={{0,1},{1,2},{2,3},{3,0},{4,5},{5,6},{6,7},{7,4},{8,9},{9,10},{10,1... | collective-permute-start | bytes 884744 | tf_op jit(solution)/shard_map/ppermute | solution.py:21
  85.7 25.4 %collective-permute-start.10 = (bf16[192,768]{1,0:T(8,128)(2,1)S(1)}, bf16[192,768]{1,0:T(8,128)(2,1)}, u32[]{:S(2)}, u32[]{:S(2)}) collective-permute-start(bf16[192,768]{1,0:T(8,128)(2,1)S(1)} %get-tuple-element.59), channel_id=1, source_target_pairs={{0,2},{1,3},{2,0},{3,1},{4,6},{5,7},{6,4},{7,5},{8,10},{9,11},{10,... | collective-permute-start | bytes 884744 | tf_op jit(solution)/shard_map/ppermute | solution.py:21
  87.0 28.9 %collective-permute-start.11 = (bf16[192,768]{1,0:T(8,128)(2,1)}, bf16[192,768]{1,0:T(8,128)(2,1)S(1)}, u32[]{:S(2)}, u32[]{:S(2)}) collective-permute-start(bf16[192,768]{1,0:T(8,128)(2,1)} %get-tuple-element.58), channel_id=1, source_target_pairs={{0,3},{1,0},{2,1},{3,2},{4,7},{5,4},{6,5},{7,6},{8,11},{9,8},{10,9... | collective-permute-start | bytes 884744 | tf_op jit(solution)/shard_map/ppermute | solution.py:21
  101.9 24.7 %collective-permute-start.21 = (bf16[192,768]{1,0:T(8,128)(2,1)}, bf16[192,768]{1,0:T(8,128)(2,1)}, u32[]{:S(2)}, u32[]{:S(2)}) collective-permute-start(bf16[192,768]{1,0:T(8,128)(2,1)} %get-tuple-element.51), channel_id=1, source_target_pairs={{0,1},{1,2},{2,3},{3,0},{4,5},{5,6},{6,7},{7,4},{8,9},{9,10},{10,1... | collective-permute-start | bytes 884744 | tf_op jit(solution)/shard_map/ppermute | solution.py:21
  111.1 83.2 %collective-permute-start.6 = (bf16[768,768]{1,0:T(8,128)(2,1)}, bf16[768,768]{1,0:T(8,128)(2,1)S(1)}, u32[]{:S(2)}, u32[]{:S(2)}) collective-permute-start(bf16[768,768]{1,0:T(8,128)(2,1)} %bitcast_select_fusion), channel_id=1, source_target_pairs={{0,24},{1,21},{2,22},{3,19},{4,28},{5,25},{6,26},{7,23},{8,0},{9,2... | collective-permute-start | bytes 3538952 | tf_op jit(solution)/shard_map/ppermute | solution.py:152
  126.7 32.9 %collective-permute-start.18 = (bf16[192,768]{1,0:T(8,128)(2,1)}, bf16[192,768]{1,0:T(8,128)(2,1)S(1)}, u32[]{:S(2)}, u32[]{:S(2)}) collective-permute-start(bf16[192,768]{1,0:T(8,128)(2,1)} %get-tuple-element.27), channel_id=1, source_target_pairs={{0,1},{1,2},{2,3},{3,0},{4,5},{5,6},{6,7},{7,4},{8,9},{9,10},{10,1... | collective-permute-start | bytes 884744 | tf_op jit(solution)/shard_map/ppermute | solution.py:21
  133.9 35.6 %collective-permute-start.19 = (bf16[192,768]{1,0:T(8,128)(2,1)}, bf16[192,768]{1,0:T(8,128)(2,1)S(1)}, u32[]{:S(2)}, u32[]{:S(2)}) collective-permute-start(bf16[192,768]{1,0:T(8,128)(2,1)} %get-tuple-element.28), channel_id=1, source_target_pairs={{0,2},{1,3},{2,0},{3,1},{4,6},{5,7},{6,4},{7,5},{8,10},{9,11},{10,... | collective-permute-start | bytes 884744 | tf_op jit(solution)/shard_map/ppermute | solution.py:21
  133.9 38.2 %collective-permute-start.20 = (bf16[192,768]{1,0:T(8,128)(2,1)}, bf16[192,768]{1,0:T(8,128)(2,1)}, u32[]{:S(2)}, u32[]{:S(2)}) collective-permute-start(bf16[192,768]{1,0:T(8,128)(2,1)} %get-tuple-element.29), channel_id=1, source_target_pairs={{0,3},{1,0},{2,1},{3,2},{4,7},{5,4},{6,5},{7,6},{8,11},{9,8},{10,9... | collective-permute-start | bytes 884744 | tf_op jit(solution)/shard_map/ppermute | solution.py:21
  148.9 45.3 %collective-permute-start.15 = (bf16[192,768]{1,0:T(8,128)(2,1)S(1)}, bf16[192,768]{1,0:T(8,128)(2,1)}, u32[]{:S(2)}, u32[]{:S(2)}) collective-permute-start(bf16[192,768]{1,0:T(8,128)(2,1)S(1)} %copy-done.10), channel_id=1, source_target_pairs={{0,1},{1,2},{2,3},{3,0},{4,5},{5,6},{6,7},{7,4},{8,9},{9,10},{10,1... | collective-permute-start | bytes 884744 | tf_op jit(solution)/shard_map/ppermute | solution.py:21
  159.5 37.1 %collective-permute-start.16 = (bf16[192,768]{1,0:T(8,128)(2,1)S(1)}, bf16[192,768]{1,0:T(8,128)(2,1)}, u32[]{:S(2)}, u32[]{:S(2)}) collective-permute-start(bf16[192,768]{1,0:T(8,128)(2,1)S(1)} %copy-done.9), channel_id=1, source_target_pairs={{0,2},{1,3},{2,0},{3,1},{4,6},{5,7},{6,4},{7,5},{8,10},{9,11},{10,... | collective-permute-start | bytes 884744 | tf_op jit(solution)/shard_map/ppermute | solution.py:21
  169.5 27.7 %collective-permute-start.17 = (bf16[192,768]{1,0:T(8,128)(2,1)S(1)}, bf16[192,768]{1,0:T(8,128)(2,1)S(1)}, u32[]{:S(2)}, u32[]{:S(2)}) collective-permute-start(bf16[192,768]{1,0:T(8,128)(2,1)S(1)} %copy-done.8), channel_id=1, source_target_pairs={{0,3},{1,0},{2,1},{3,2},{4,7},{5,4},{6,5},{7,6},{8,11},{9,8},{10,9... | collective-permute-start | bytes 884744 | tf_op jit(solution)/shard_map/ppermute | solution.py:21
  172.1 34.9 %collective-permute-start.30 = (bf16[192,768]{1,0:T(8,128)(2,1)}, bf16[192,768]{1,0:T(8,128)(2,1)S(1)}, u32[]{:S(2)}, u32[]{:S(2)}) collective-permute-start(bf16[192,768]{1,0:T(8,128)(2,1)} %get-tuple-element.36), channel_id=1, source_target_pairs={{0,1},{1,2},{2,3},{3,0},{4,5},{5,6},{6,7},{7,4},{8,9},{9,10},{10,1... | collective-permute-start | bytes 884744 | tf_op jit(solution)/shard_map/ppermute | solution.py:21
  194.2 26.1 %collective-permute-start.31 = (bf16[192,768]{1,0:T(8,128)(2,1)}, bf16[192,768]{1,0:T(8,128)(2,1)}, u32[]{:S(2)}, u32[]{:S(2)}) collective-permute-start(bf16[192,768]{1,0:T(8,128)(2,1)} %get-tuple-element.37), channel_id=1, source_target_pairs={{0,2},{1,3},{2,0},{3,1},{4,6},{5,7},{6,4},{7,5},{8,10},{9,11},{10,... | collective-permute-start | bytes 884744 | tf_op jit(solution)/shard_map/ppermute | solution.py:21
  194.2 30.1 %collective-permute-start.32 = (bf16[192,768]{1,0:T(8,128)(2,1)}, bf16[192,768]{1,0:T(8,128)(2,1)}, u32[]{:S(2)}, u32[]{:S(2)}) collective-permute-start(bf16[192,768]{1,0:T(8,128)(2,1)} %get-tuple-element.38), channel_id=1, source_target_pairs={{0,3},{1,0},{2,1},{3,2},{4,7},{5,4},{6,5},{7,6},{8,11},{9,8},{10,9... | collective-permute-start | bytes 884744 | tf_op jit(solution)/shard_map/ppermute | solution.py:21
  196.6 31.1 %collective-permute-start.27 = (bf16[192,768]{1,0:T(8,128)(2,1)}, bf16[192,768]{1,0:T(8,128)(2,1)S(1)}, u32[]{:S(2)}, u32[]{:S(2)}) collective-permute-start(bf16[192,768]{1,0:T(8,128)(2,1)} %get-tuple-element.33), channel_id=1, source_target_pairs={{0,1},{1,2},{2,3},{3,0},{4,5},{5,6},{6,7},{7,4},{8,9},{9,10},{10,1... | collective-permute-start | bytes 884744 | tf_op jit(solution)/shard_map/ppermute | solution.py:21
  197.3 48.3 %collective-permute-start.28 = (bf16[192,768]{1,0:T(8,128)(2,1)S(1)}, bf16[192,768]{1,0:T(8,128)(2,1)S(1)}, u32[]{:S(2)}, u32[]{:S(2)}) collective-permute-start(bf16[192,768]{1,0:T(8,128)(2,1)S(1)} %copy-done.12), channel_id=1, source_target_pairs={{0,2},{1,3},{2,0},{3,1},{4,6},{5,7},{6,4},{7,5},{8,10},{9,11},{10,... | collective-permute-start | bytes 884744 | tf_op jit(solution)/shard_map/ppermute | solution.py:21
  207.0 38.6 %collective-permute-start.29 = (bf16[192,768]{1,0:T(8,128)(2,1)S(1)}, bf16[192,768]{1,0:T(8,128)(2,1)}, u32[]{:S(2)}, u32[]{:S(2)}) collective-permute-start(bf16[192,768]{1,0:T(8,128)(2,1)S(1)} %copy-done.11), channel_id=1, source_target_pairs={{0,3},{1,0},{2,1},{3,2},{4,7},{5,4},{6,5},{7,6},{8,11},{9,8},{10,9... | collective-permute-start | bytes 884744 | tf_op jit(solution)/shard_map/ppermute | solution.py:21
  220.3 33.9 %collective-permute-start.24 = (bf16[192,768]{1,0:T(8,128)(2,1)S(1)}, bf16[192,768]{1,0:T(8,128)(2,1)S(1)}, u32[]{:S(2)}, u32[]{:S(2)}) collective-permute-start(bf16[192,768]{1,0:T(8,128)(2,1)S(1)} %copy-done.7), channel_id=1, source_target_pairs={{0,1},{1,2},{2,3},{3,0},{4,5},{5,6},{6,7},{7,4},{8,9},{9,10},{10,1... | collective-permute-start | bytes 884744 | tf_op jit(solution)/shard_map/ppermute | solution.py:21
  224.3 33.8 %collective-permute-start.25 = (bf16[192,768]{1,0:T(8,128)(2,1)S(1)}, bf16[192,768]{1,0:T(8,128)(2,1)S(1)}, u32[]{:S(2)}, u32[]{:S(2)}) collective-permute-start(bf16[192,768]{1,0:T(8,128)(2,1)S(1)} %copy-done.6), channel_id=1, source_target_pairs={{0,2},{1,3},{2,0},{3,1},{4,6},{5,7},{6,4},{7,5},{8,10},{9,11},{10,... | collective-permute-start | bytes 884744 | tf_op jit(solution)/shard_map/ppermute | solution.py:21
  227.7 30.5 %collective-permute-start.26 = (bf16[192,768]{1,0:T(8,128)(2,1)S(1)}, bf16[192,768]{1,0:T(8,128)(2,1)S(1)}, u32[]{:S(2)}, u32[]{:S(2)}) collective-permute-start(bf16[192,768]{1,0:T(8,128)(2,1)S(1)} %copy-done.5), channel_id=1, source_target_pairs={{0,3},{1,0},{2,1},{3,2},{4,7},{5,4},{6,5},{7,6},{8,11},{9,8},{10,9... | collective-permute-start | bytes 884744 | tf_op jit(solution)/shard_map/ppermute | solution.py:21
  273.6 28.8 %collective-permute-start.35 = (bf16[208,768]{1,0:T(8,128)(2,1)}, bf16[208,768]{1,0:T(8,128)(2,1)S(1)}, u32[]{:S(2)}, u32[]{:S(2)}) collective-permute-start(bf16[208,768]{1,0:T(8,128)(2,1)} %get-tuple-element.41), channel_id=1, source_target_pairs={{0,2},{1,7},{2,4},{3,9},{4,6},{5,11},{6,8},{7,13},{8,10},{9,15},{1... | collective-permute-start | bytes 958472 | tf_op jit(solution)/shard_map/ppermute | solution.py:181
  273.6 28.9 %collective-permute-start.34 = (bf16[208,768]{1,0:T(8,128)(2,1)}, bf16[208,768]{1,0:T(8,128)(2,1)S(1)}, u32[]{:S(2)}, u32[]{:S(2)}) collective-permute-start(bf16[208,768]{1,0:T(8,128)(2,1)} %get-tuple-element.40), channel_id=1, source_target_pairs={{0,1},{1,6},{2,7},{3,8},{4,5},{5,10},{6,11},{7,12},{8,9},{9,14},{1... | collective-permute-start | bytes 958472 | tf_op jit(solution)/shard_map/ppermute | solution.py:181
  273.7 28.9 %collective-permute-start.33 = (bf16[208,768]{1,0:T(8,128)(2,1)}, bf16[208,768]{1,0:T(8,128)(2,1)S(1)}, u32[]{:S(2)}, u32[]{:S(2)}) collective-permute-start(bf16[208,768]{1,0:T(8,128)(2,1)} %get-tuple-element.39), channel_id=1, source_target_pairs={{0,0},{1,5},{2,6},{3,11},{4,4},{5,9},{6,10},{7,15},{8,8},{9,13},{1... | collective-permute-start | bytes 958472 | tf_op jit(solution)/shard_map/ppermute | solution.py:181
  (30 other events, 338.4 us)
where the time goes:
time: 304 us
  starting transfers between devices  124 us (41%)
  waiting for transfers between devices  90.4 us (30%)
  Pallas kernels  63.4 us (21%)
  other arithmetic  15.4 us (5%)
  local copies, waits for them, and re-layouts  10.4 us (3%)
    ppermute x30, starting transfers between devices, rotate(): lax.ppermute(block, axis, [(i, (i + distance) % size) for i in range(size)])  111 us
    pallas_call x8, Pallas kernels, one_block(): pl.pallas_call(functools.partial(block_kernel, groups, first, last, scale...  63.4 us
    ppermute x30, waiting for transfers between devices, rotate(): lax.ppermute(block, axis, [(i, (i + distance) % size) for i in range(size)])  63.3 us
    ppermute x4, waiting for transfers between devices, body(): part = lax.ppermute(total[s], ('sec', 'blk'), route).astype(jnp.float32)  27.1 us
    ppermute x4, starting transfers between devices, body(): part = lax.ppermute(total[s], ('sec', 'blk'), route).astype(jnp.float32)  8.33 us
    squeeze x2, local copies, waits for them, and re-layouts, body(): lax.dynamic_index_in_dim(two_site, ahead[s] * here + c, 0, keepdims=False)  7.34 us
  transfers between devices with their start and end apart: 37, of which 12 were waited for; matrix products, arithmetic and copies ran while one was open for 6% of the time, Pallas kernels for 18%

commit v1 on v0

--- a/solution.py
+++ b/solution.py
@@ -9,7 +9,7 @@
 STATES = 2
 PAIRS = 16
 PAD = 16
-WINDOW = 3
+WINDOW = 5
 
 
 def charge(level):
@@ -76,13 +76,13 @@
             sends[s][rows:, :] = jnp.broadcast_to(gap, (PAD, width)).astype(jnp.bfloat16)
 
 
-def one_block(z, left, right, two_site, own_base, pieces, before, last, scale):
+def one_block(z, left, right, two_site, c, here, pieces, before, last, scale):
     groups = len(pieces) + 1
     rows, width = pieces[0].shape
     first = before is None
     whole = pl.BlockSpec((width, width), lambda i, w: (0, 0))
     piece_spec = pl.BlockSpec((1, rows, width), lambda i, w: (0, 0, 0))
-    own_spec = pl.BlockSpec((1, rows, width), lambda i, w: (w[1], 0, 0))
+    own_spec = pl.BlockSpec((1, rows, width), lambda i, w: (w[0] * here + c, 0, 0))
     in_specs = [whole, whole, own_spec] + [piece_spec] * (groups - 1)
     operands = [left, right, two_site] + [p[None] for p in pieces]
     if not first:
@@ -110,13 +110,26 @@
             flops=6 * width**3, transcendentals=0, bytes_accessed=12 * width * width
         ),
         name="last_block" if last else "one_block",
-    )(jnp.stack([z, own_base]), *operands)
+    )(z.astype(jnp.int32)[None], *operands)
 
 
 def named(block, distance):
-    if not distance:
-        return block
     return rotate(block, "blk", distance)
+
+
+def forward(block, step, up):
+    last = lax.axis_size("blk") - 1
+    route = [(i, i + 1) for i in range(step - 1, last)]
+    if not up:
+        route = [(last - i, last - j) for i, j in route]
+    return lax.ppermute(block, "blk", route)
+
+
+def in_order(from_below, from_above, blk_index):
+    rows, width = from_below[0].shape
+    groups = len(from_below)
+    line = jnp.concatenate(from_below[:0:-1] + from_above, axis=0)
+    return lax.dynamic_slice(line, ((groups - 1 - blk_index) * rows, 0), (groups * rows, width))
 
 
 def body(two_site, left_env, right_env, left_size, right_size):
@@ -127,16 +140,42 @@
     total_blocks, rows, width = two_site.shape
     pairs_here = PAIRS // groups
     here = total_blocks // groups
-    behind = [(blk_index - s) % groups for s in range(groups)]
     ahead = [(blk_index + s) % groups for s in range(groups)]
 
+    right_own = live_rows(right_env[0], pick_value(right_size, sec_index), blk_index * rows)
     left_own = live_rows(left_env[0], pick_value(left_size, sec_index), blk_index * rows)
-    left_parts = [named(left_own, s) for s in range(groups)]
-    right_own = live_rows(right_env[0], pick_value(right_size, sec_index), blk_index * rows)
-    right_parts = [named(right_own, s) for s in range(groups)]
-    left_full = jnp.concatenate(left_parts, axis=0)
-    right_full = jnp.take(jnp.stack(right_parts), jnp.stack(behind), axis=0)
-    right_full = right_full.reshape(width, width)
+    right_up, right_down = [right_own], [right_own]
+    left_up, left_down = [left_own], [left_own]
+
+    def send(c, *after):
+        pieces = [
+            lax.dynamic_index_in_dim(two_site, ahead[s] * here + c, 0, keepdims=False)
+            for s in range(1, groups)
+        ]
+        if after:
+            pieces, after = lax.optimization_barrier((pieces, after))
+        return [named(p, s + 1) for s, p in enumerate(pieces)], after
+
+    chunks = []
+    for t in range(groups):
+        if t < groups - 1:
+            right_up.append(forward(right_up[t], t + 1, True))
+            right_down.append(forward(right_down[t], t + 1, False))
+        if t:
+            left_up.append(forward(left_up[t - 1], t, True))
+            left_down.append(forward(left_down[t - 1], t, False))
+        if t < here:
+            if t:
+                sent, (right_up[t], right_down[t]) = send(t, right_up[t], right_down[t])
+            else:
+                sent, _ = send(t)
+            chunks.append(sent)
+    right_full = in_order(right_up, right_down, blk_index)
+    if here > groups:
+        last = groups - 1
+        sent, (left_up[last], left_down[last]) = send(groups, left_up[last], left_down[last])
+        chunks.append(sent)
+    left_full = in_order(left_up, left_down, blk_index)
 
     right_of = []
     arrived = {}
@@ -154,17 +193,13 @@
 
     totals = []
     for c in range(here):
-        pieces = [
-            lax.dynamic_index_in_dim(two_site, ahead[s] * here + c, 0, keepdims=False)
-            for s in range(1, groups)
-        ]
-        if c >= WINDOW:
-            pieces, totals[c - WINDOW] = lax.optimization_barrier((pieces, totals[c - WINDOW]))
-        pieces = [named(p, s + 1) for s, p in enumerate(pieces)]
+        if c >= len(chunks):
+            sent, (totals[c - WINDOW],) = send(c, totals[c - WINDOW])
+            chunks.append(sent)
         totals.append(
             one_block(
-                blk_index, left_full, right_of[c // STATES], two_site, blk_index * here + c,
-                pieces, totals[-1] if c else None, c == here - 1, 1.0 / (8.0 * width),
+                blk_index, left_full, right_of[c // STATES], two_site, c, here,
+                chunks[c], totals[-1] if c else None, c == here - 1, 1.0 / (8.0 * width),
             )
         )
     total = totals[-1]

time: 304 us -> 301 us (level)
  waiting for transfers between devices: 90.4 us -> 113 us
  starting transfers between devices: 124 us -> 111 us
  other arithmetic: 15.4 us -> 7.88 us
  Pallas kernels: 63.4 us -> 58.1 us
    ppermute x30 -> x24, starting transfers between devices: 111 us -> 77.3 us  [rotate(): lax.ppermute(block, axis, [(i, (i + distance) % size) for i in range(size)])]
    ppermute x0 -> x12, starting transfers between devices: none -> 20 us  [forward(): return lax.ppermute(block, 'blk', route)]
    ppermute x0 -> x12, waiting for transfers between devices: none -> 17.2 us  [forward(): return lax.ppermute(block, 'blk', route)]
    pallas_call x8, Pallas kernels: 63.4 us -> 58.1 us  [one_block(): pl.pallas_call(functools.partial(block_kernel, groups, first, last, scale...]
    another operation x9 -> x0, other arithmetic: 5.21 us -> none  [the longest x8 5.06 us: one_block(): jnp.stack([z, own_base])]
    ppermute x30 -> x24, waiting for transfers between devices: 63.3 us -> 67.1 us  [rotate(): lax.ppermute(block, axis, [(i, (i + distance) % size) for i in range(size)])]
  transfers between devices with their start and end apart: 37 -> 43, of which waited for: 12 -> 14; matrix products, arithmetic and copies ran while one was open for 6% -> 4% of each run, Pallas kernels for 18% -> 17%
where the time goes in v1:
time: 301 us; the launch traced here: 300 us
  waiting for transfers between devices  113 us (38%)
  starting transfers between devices  111 us (37%)
  Pallas kernels  58.1 us (19%)
  local copies, waits for them, and re-layouts  10.3 us (3%)
  other arithmetic  7.88 us (3%)
    ppermute x24, starting transfers between devices, rotate(): lax.ppermute(block, axis, [(i, (i + distance) % size) for i in range(size)])  77.3 us
    ppermute x24, waiting for transfers between devices, rotate(): lax.ppermute(block, axis, [(i, (i + distance) % size) for i in range(size)])  67.1 us
    pallas_call x8, Pallas kernels, one_block(): pl.pallas_call(functools.partial(block_kernel, groups, first, last, scale...  58.1 us
    ppermute x4, waiting for transfers between devices, body(): part = lax.ppermute(total[s], ('sec', 'blk'), route).astype(jnp.float32)  28.2 us
    ppermute x12, starting transfers between devices, forward(): return lax.ppermute(block, 'blk', route)  20 us
    ppermute x12, waiting for transfers between devices, forward(): return lax.ppermute(block, 'blk', route)  17.2 us
    ppermute x4, starting transfers between devices, body(): part = lax.ppermute(total[s], ('sec', 'blk'), route).astype(jnp.float32)  8.15 us
    squeeze x2, local copies, waits for them, and re-layouts, send(): lax.dynamic_index_in_dim(two_site, ahead[s] * here + c, 0, keepdims=False)  6.69 us
  transfers between devices with their start and end apart: 43, of which 14 were waited for; matrix products, arithmetic and copies ran while one was open for 4% of the time, Pallas kernels for 17%

profile of v1, /device:TPU:0, one launch (start us, length us, event | category | flops | bytes accessed | tf_op | source)
XLA Modules:
  0.0 300.4 jit_solution(879137160522236151)
XLA Ops:
  5.2 5.6 %collective-permute-start.6 = (bf16[192,768]{1,0:T(8,128)(2,1)S(1)}, bf16[192,768]{1,0:T(8,128)(2,1)S(1)}, u32[]{:S(2)}, u32[]{:S(2)}) collective-permute-start(bf16[192,768]{1,0:T(8,128)(2,1)S(1)} %and_select_fusion), channel_id=1, source_target_pairs={{0,1},{1,2},{2,3},{4,5},{5,6},{6,7},{8,9},{9,10},{10,11},{12,13},{... | collective-permute-start | bytes 884744 | tf_op jit(solution)/shard_map/ppermute | solution.py:125
  13.2 3.9 %collective-permute-start = (bf16[192,768]{1,0:T(8,128)(2,1)S(1)}, bf16[192,768]{1,0:T(8,128)(2,1)S(1)}, u32[]{:S(2)}, u32[]{:S(2)}) collective-permute-start(bf16[192,768]{1,0:T(8,128)(2,1)S(1)} %and_select_fusion.1), channel_id=1, source_target_pairs={{0,1},{1,2},{2,3},{4,5},{5,6},{6,7},{8,9},{9,10},{10,11},{12,13},{... | collective-permute-start | bytes 884744 | tf_op jit(solution)/shard_map/ppermute | solution.py:125
  24.0 4.9 %collective-permute-done.3 = bf16[192,768]{1,0:T(8,128)(2,1)S(1)} collective-permute-done((bf16[192,768]{1,0:T(8,128)(2,1)S(1)}, bf16[192,768]{1,0:T(8,128)(2,1)S(1)}, u32[]{:S(2)}, u32[]{:S(2)}) %collective-permute-start.3) | collective-permute-done | bytes 294944 | tf_op jit(solution)/shard_map/ppermute | solution.py:125
  30.2 5.0 %collective-permute-done.10 = bf16[192,768]{1,0:T(8,128)(2,1)S(1)} collective-permute-done((bf16[192,768]{1,0:T(8,128)(2,1)S(1)}, bf16[192,768]{1,0:T(8,128)(2,1)S(1)}, u32[]{:S(2)}, u32[]{:S(2)}) %collective-permute-start.10) | collective-permute-done | bytes 294944 | tf_op jit(solution)/shard_map/ppermute | solution.py:125
  39.9 4.0 %dynamic-slice_bitcast_fusion = (bf16[192,768]{1,0:T(8,128)(2,1)}, bf16[192,768]{1,0:T(8,128)(2,1)}, bf16[192,768]{1,0:T(8,128)(2,1)}, bf16[192,768]{1,0:T(8,128...) fusion(bf16[32,192,768]{2,1,0:T(8,128)(2,1)} %refs_2_.15, ...), kind=kLoop, calls=%fused_computation.11 | loop fusion | bytes 10616904 | tf_op jit(solution)/shard_map/jit(dynamic_index_in_dim)/squeeze | solution.py:152
  55.0 3.9 %collective-permute-done.5 = bf16[192,768]{1,0:T(8,128)(2,1)S(1)} collective-permute-done((bf16[192,768]{1,0:T(8,128)(2,1)S(1)}, bf16[192,768]{1,0:T(8,128)(2,1)S(1)}, u32[]{:S(2)}, u32[]{:S(2)}) %collective-permute-start.5) | collective-permute-done | bytes 294944 | tf_op jit(solution)/shard_map/ppermute | solution.py:125
  58.9 3.4 %collective-permute-done.21 = bf16[192,768]{1,0:T(8,128)(2,1)S(1)} collective-permute-done((bf16[192,768]{1,0:T(8,128)(2,1)S(1)}, bf16[192,768]{1,0:T(8,128)(2,1)S(1)}, u32[]{:S(2)}, u32[]{:S(2)}) %collective-permute-start.21) | collective-permute-done | bytes 294944 | tf_op jit(solution)/shard_map/ppermute | solution.py:21
  62.6 19.5 %collective-permute-done.22 = bf16[192,768]{1,0:T(8,128)(2,1)S(1)} collective-permute-done((bf16[192,768]{1,0:T(8,128)(2,1)S(1)}, bf16[192,768]{1,0:T(8,128)(2,1)S(1)}, u32[]{:S(2)}, u32[]{:S(2)}) %collective-permute-start.22) | collective-permute-done | bytes 294944 | tf_op jit(solution)/shard_map/ppermute | solution.py:21
  82.1 11.3 %collective-permute-start.14 = (bf16[192,768]{1,0:T(8,128)(2,1)S(1)}, bf16[192,768]{1,0:T(8,128)(2,1)}, u32[]{:S(2)}, u32[]{:S(2)}) collective-permute-start(bf16[192,768]{1,0:T(8,128)(2,1)S(1)} %get-tuple-element.46), channel_id=1, source_target_pairs={{0,1},{1,2},{2,3},{3,0},{4,5},{5,6},{6,7},{7,4},{8,9},{9,10},{10,1... | collective-permute-start | bytes 884744 | tf_op jit(solution)/shard_map/ppermute | solution.py:21
  94.6 8.6 %collective-permute-done.19 = bf16[192,768]{1,0:T(8,128)(2,1)S(1)} collective-permute-done((bf16[192,768]{1,0:T(8,128)(2,1)S(1)}, bf16[192,768]{1,0:T(8,128)(2,1)S(1)}, u32[]{:S(2)}, u32[]{:S(2)}) %collective-permute-start.19) | collective-permute-done | bytes 294944 | tf_op jit(solution)/shard_map/ppermute | solution.py:21
  103.2 3.6 %collective-permute-start.16 = (bf16[192,768]{1,0:T(8,128)(2,1)S(1)}, bf16[192,768]{1,0:T(8,128)(2,1)S(1)}, u32[]{:S(2)}, u32[]{:S(2)}) collective-permute-start(bf16[192,768]{1,0:T(8,128)(2,1)S(1)} %get-tuple-element.48), channel_id=1, source_target_pairs={{0,3},{1,0},{2,1},{3,2},{4,7},{5,4},{6,5},{7,6},{8,11},{9,8},{10,9... | collective-permute-start | bytes 884744 | tf_op jit(solution)/shard_map/ppermute | solution.py:21
  109.4 12.8 %collective-permute-done.15 = bf16[192,768]{1,0:T(8,128)(2,1)S(1)} collective-permute-done((bf16[192,768]{1,0:T(8,128)(2,1)S(1)}, bf16[192,768]{1,0:T(8,128)(2,1)S(1)}, u32[]{:S(2)}, u32[]{:S(2)}) %collective-permute-start.15) | collective-permute-done | bytes 294944 | tf_op jit(solution)/shard_map/ppermute | solution.py:21
  122.2 6.8 %collective-permute-start.36 = (bf16[192,768]{1,0:T(8,128)(2,1)}, bf16[192,768]{1,0:T(8,128)(2,1)}, u32[]{:S(2)}, u32[]{:S(2)}) collective-permute-start(bf16[192,768]{1,0:T(8,128)(2,1)} %get-tuple-element.64), channel_id=1, source_target_pairs={{0,1},{1,2},{2,3},{3,0},{4,5},{5,6},{6,7},{7,4},{8,9},{9,10},{10,1... | collective-permute-start | bytes 884744 | tf_op jit(solution)/shard_map/ppermute | solution.py:21
  129.0 3.4 %collective-permute-start.37 = (bf16[192,768]{1,0:T(8,128)(2,1)}, bf16[192,768]{1,0:T(8,128)(2,1)}, u32[]{:S(2)}, u32[]{:S(2)}) collective-permute-start(bf16[192,768]{1,0:T(8,128)(2,1)} %get-tuple-element.65), channel_id=1, source_target_pairs={{0,2},{1,3},{2,0},{3,1},{4,6},{5,7},{6,4},{7,5},{8,10},{9,11},{10,... | collective-permute-start | bytes 884744 | tf_op jit(solution)/shard_map/ppermute | solution.py:21
  133.9 6.5 %one_block.7.refs_6_ = f32[768,768]{1,0:T(8,128)} custom-call(s32[1]{0:T(128)} %bitcast.where_ref, bf16[768,768]{1,0:T(8,128)(2,1)} %constant_dynamic-slice_fusion.1.refs_0_, bf16[768,768]{1,0:T(8,128)(2,1)} %copy-done.2, bf16[32,192,768]{2,1,0:T(8,128)(2,1)} %refs_2_.15, bf16[1,192,768]{2,1,0:T(8,128)(2,1)} %bitcast.84, bf16[1,192,768]{2,1,0:T(8,128)(2,1)} %bitcast.86, ...), custom_call_target="tpu_custom_call" | custom-call | flops 2717908992 | bytes 7077888 | tf_op jit(solution)/shard_map/one_block/pallas_call | solution.py:101
  142.2 10.6 %collective-permute-done.37 = bf16[192,768]{1,0:T(8,128)(2,1)} collective-permute-done((bf16[192,768]{1,0:T(8,128)(2,1)}, bf16[192,768]{1,0:T(8,128)(2,1)}, u32[]{:S(2)}, u32[]{:S(2)}) %collective-permute-start.37) | collective-permute-done | bytes 294944 | tf_op jit(solution)/shard_map/ppermute | solution.py:21
  152.8 6.4 %collective-permute-start.35 = (bf16[192,768]{1,0:T(8,128)(2,1)}, bf16[192,768]{1,0:T(8,128)(2,1)}, u32[]{:S(2)}, u32[]{:S(2)}) collective-permute-start(bf16[192,768]{1,0:T(8,128)(2,1)} %get-tuple-element.63), channel_id=1, source_target_pairs={{0,3},{1,0},{2,1},{3,2},{4,7},{5,4},{6,5},{7,6},{8,11},{9,8},{10,9... | collective-permute-start | bytes 884744 | tf_op jit(solution)/shard_map/ppermute | solution.py:21
  159.2 7.4 %one_block.8.refs_6_ = f32[768,768]{1,0:T(8,128)} custom-call(s32[1]{0:T(128)} %bitcast.where_ref, bf16[768,768]{1,0:T(8,128)(2,1)} %constant_dynamic-slice_fusion.1.refs_0_, bf16[768,768]{1,0:T(8,128)(2,1)} %copy-done.2, bf16[32,192,768]{2,1,0:T(8,128)(2,1)} %refs_2_.15, bf16[1,192,768]{2,1,0:T(8,128)(2,1)} %bitcast.83, ...), custom_call_target="tpu_custom_call", output_to_operand_aliasing={{}: (7, {})} | custom-call | flops 2717908992 | bytes 7077888 | tf_op jit(solution)/shard_map/one_block/pallas_call | solution.py:101
  166.5 12.6 %collective-permute-start.30 = (bf16[192,768]{1,0:T(8,128)(2,1)S(1)}, bf16[192,768]{1,0:T(8,128)(2,1)S(1)}, u32[]{:S(2)}, u32[]{:S(2)}) collective-permute-start(bf16[192,768]{1,0:T(8,128)(2,1)S(1)} %copy-done.10), channel_id=1, source_target_pairs={{0,1},{1,2},{2,3},{3,0},{4,5},{5,6},{6,7},{7,4},{8,9},{9,10},{10,1... | collective-permute-start | bytes 884744 | tf_op jit(solution)/shard_map/ppermute | solution.py:21
  179.2 7.3 %one_block.9.refs_6_ = f32[768,768]{1,0:T(8,128)} custom-call(s32[1]{0:T(128)} %bitcast.where_ref, bf16[768,768]{1,0:T(8,128)(2,1)} %constant_dynamic-slice_fusion.1.refs_0_, bf16[768,768]{1,0:T(8,128)(2,1)} %copy-done, bf16[32,192,768]{2,1,0:T(8,128)(2,1)} %refs_2_.15, bf16[1,192,768]{2,1,0:T(8,128)(2,1)} %bitcast.18.refs_3_, ...), custom_call_target="tpu_custom_call", output_to_operand_aliasing={{}: (7, {})} | custom-call | flops 2717908992 | bytes 7077888 | tf_op jit(solution)/shard_map/one_block/pallas_call | solution.py:101
  190.9 7.4 %one_block.10.refs_6_ = f32[768,768]{1,0:T(8,128)} custom-call(s32[1]{0:T(128)} %bitcast.where_ref, bf16[768,768]{1,0:T(8,128)(2,1)} %constant_dynamic-slice_fusion.1.refs_0_, bf16[768,768]{1,0:T(8,128)(2,1)} %copy-done, bf16[32,192,768]{2,1,0:T(8,128)(2,1)} %refs_2_.15, bf16[1,192,768]{2,1,0:T(8,128)(2,1)} %bitcast.48.refs_3_, ...), custom_call_target="tpu_custom_call", output_to_operand_aliasing={{}: (7, {})} | custom-call | flops 2717908992 | bytes 7077888 | tf_op jit(solution)/shard_map/one_block/pallas_call | solution.py:101
  202.3 7.4 %one_block.11.refs_6_ = f32[768,768]{1,0:T(8,128)} custom-call(s32[1]{0:T(128)} %bitcast.where_ref, bf16[768,768]{1,0:T(8,128)(2,1)} %constant_dynamic-slice_fusion.1.refs_0_, bf16[768,768]{1,0:T(8,128)(2,1)} %copy-done, bf16[32,192,768]{2,1,0:T(8,128)(2,1)} %refs_2_.15, bf16[1,192,768]{2,1,0:T(8,128)(2,1)} %bitcast.92, ...), custom_call_target="tpu_custom_call", output_to_operand_aliasing={{}: (7, {})} | custom-call | flops 2717908992 | bytes 7077888 | tf_op jit(solution)/shard_map/one_block/pallas_call | solution.py:101
  211.0 12.4 %collective-permute-start.25 = (bf16[192,768]{1,0:T(8,128)(2,1)S(1)}, bf16[192,768]{1,0:T(8,128)(2,1)S(1)}, u32[]{:S(2)}, u32[]{:S(2)}) collective-permute-start(bf16[192,768]{1,0:T(8,128)(2,1)S(1)} %copy-done.6), channel_id=1, source_target_pairs={{0,2},{1,3},{2,0},{3,1},{4,6},{5,7},{6,4},{7,5},{8,10},{9,11},{10,... | collective-permute-start | bytes 884744 | tf_op jit(solution)/shard_map/ppermute | solution.py:21
  223.5 4.0 %collective-permute-start.26 = (bf16[192,768]{1,0:T(8,128)(2,1)S(1)}, bf16[192,768]{1,0:T(8,128)(2,1)S(1)}, u32[]{:S(2)}, u32[]{:S(2)}) collective-permute-start(bf16[192,768]{1,0:T(8,128)(2,1)S(1)} %copy-done.5), channel_id=1, source_target_pairs={{0,3},{1,0},{2,1},{3,2},{4,7},{5,4},{6,5},{7,6},{8,11},{9,8},{10,9... | collective-permute-start | bytes 884744 | tf_op jit(solution)/shard_map/ppermute | solution.py:21
  227.5 7.3 %one_block.12.refs_6_ = f32[768,768]{1,0:T(8,128)} custom-call(s32[1]{0:T(128)} %bitcast.where_ref, bf16[768,768]{1,0:T(8,128)(2,1)} %constant_dynamic-slice_fusion.1.refs_0_, bf16[768,768]{1,0:T(8,128)(2,1)} %copy-done, bf16[32,192,768]{2,1,0:T(8,128)(2,1)} %refs_2_.15, bf16[1,192,768]{2,1,0:T(8,128)(2,1)} %bitcast.91, ...), custom_call_target="tpu_custom_call", output_to_operand_aliasing={{}: (7, {})} | custom-call | flops 2717908992 | bytes 7077888 | tf_op jit(solution)/shard_map/one_block/pallas_call | solution.py:101
  234.9 6.9 %collective-permute-done.28 = bf16[192,768]{1,0:T(8,128)(2,1)} collective-permute-done((bf16[192,768]{1,0:T(8,128)(2,1)S(1)}, bf16[192,768]{1,0:T(8,128)(2,1)}, u32[]{:S(2)}, u32[]{:S(2)}) %collective-permute-start.28) | collective-permute-done | bytes 294944 | tf_op jit(solution)/shard_map/ppermute | solution.py:21
  241.8 7.3 %one_block.13.refs_6_ = f32[768,768]{1,0:T(8,128)} custom-call(s32[1]{0:T(128)} %bitcast.where_ref, bf16[768,768]{1,0:T(8,128)(2,1)} %constant_dynamic-slice_fusion.1.refs_0_, bf16[768,768]{1,0:T(8,128)(2,1)} %copy-done.1, bf16[32,192,768]{2,1,0:T(8,128)(2,1)} %refs_2_.15, bf16[1,192,768]{2,1,0:T(8,128)(2,1)} %bitcast.95, ...), custom_call_target="tpu_custom_call", output_to_operand_aliasing={{}: (7, {})} | custom-call | flops 2717908992 | bytes 7077888 | tf_op jit(solution)/shard_map/one_block/pallas_call | solution.py:101
  249.1 5.2 %collective-permute-done.25 = bf16[192,768]{1,0:T(8,128)(2,1)S(1)} collective-permute-done((bf16[192,768]{1,0:T(8,128)(2,1)S(1)}, bf16[192,768]{1,0:T(8,128)(2,1)S(1)}, u32[]{:S(2)}, u32[]{:S(2)}) %collective-permute-start.25) | collective-permute-done | bytes 294944 | tf_op jit(solution)/shard_map/ppermute | solution.py:21
  255.1 7.4 %last_block.1 = (bf16[208,768]{1,0:T(8,128)(2,1)}, bf16[208,768]{1,0:T(8,128)(2,1)}, bf16[208,768]{1,0:T(8,128)(2,1)}, bf16[208,768]{1,0:T(8,128)(2,1)}) custom-call(s32[1]{0:T(128)} %bitcast.where_ref, bf16[768,768]{1,0:T(8,128)(2,1)} %constant_dynamic-slice_fusion.1.refs_0_, bf16[768,768]{1,0:T(8,128)(2,1)} %copy-done.1, bf16[32,192,768]{2,1,0:T(8,128)(2,1)} %refs_2_.15, ...), custom_call_target="tpu_custom_call" | custom-call | flops 2717908992 | bytes 7077888 | tf_op jit(solution)/shard_map/last_block/pallas_call | solution.py:101
  262.6 6.5 %collective-permute-start.42 = (bf16[208,768]{1,0:T(8,128)(2,1)}, bf16[208,768]{1,0:T(8,128)(2,1)S(1)}, u32[]{:S(2)}, u32[]{:S(2)}) collective-permute-start(bf16[208,768]{1,0:T(8,128)(2,1)} %get-tuple-element.70), channel_id=1, source_target_pairs={{0,3},{1,4},{2,5},{3,10},{4,7},{5,8},{6,9},{7,14},{8,11},{9,12},{1... | collective-permute-start | bytes 958472 | tf_op jit(solution)/shard_map/ppermute | solution.py:216
  270.7 6.6 %collective-permute-done.42 = bf16[208,768]{1,0:T(8,128)(2,1)S(1)} collective-permute-done((bf16[208,768]{1,0:T(8,128)(2,1)}, bf16[208,768]{1,0:T(8,128)(2,1)S(1)}, u32[]{:S(2)}, u32[]{:S(2)}) %collective-permute-start.42) | collective-permute-done | bytes 319520 | tf_op jit(solution)/shard_map/ppermute | solution.py:216
  277.4 21.6 %collective-permute-done.41 = bf16[208,768]{1,0:T(8,128)(2,1)S(1)} collective-permute-done((bf16[208,768]{1,0:T(8,128)(2,1)}, bf16[208,768]{1,0:T(8,128)(2,1)S(1)}, u32[]{:S(2)}, u32[]{:S(2)}) %collective-permute-start.41) | collective-permute-done | bytes 319520 | tf_op jit(solution)/shard_map/ppermute | solution.py:216
  (157 shorter events, 52.0 us)
Async XLA Ops:
  18.5 16.8 %collective-permute-start.10 = (bf16[192,768]{1,0:T(8,128)(2,1)S(1)}, bf16[192,768]{1,0:T(8,128)(2,1)S(1)}, u32[]{:S(2)}, u32[]{:S(2)}) collective-permute-start(bf16[192,768]{1,0:T(8,128)(2,1)S(1)} %collective-permute-done.9), channel_id=1, source_target_pairs={{2,1},{1,0},{6,5},{5,4},{10,9},{9,8},{14,13},{13,12},{18,17},{17,1... | collective-permute-start | bytes 884744 | tf_op jit(solution)/shard_map/ppermute | solution.py:125
  19.8 16.8 %collective-permute-start.7 = (bf16[192,768]{1,0:T(8,128)(2,1)S(1)}, bf16[192,768]{1,0:T(8,128)(2,1)S(1)}, u32[]{:S(2)}, u32[]{:S(2)}) collective-permute-start(bf16[192,768]{1,0:T(8,128)(2,1)S(1)} %collective-permute-done.6), channel_id=1, source_target_pairs={{1,2},{2,3},{5,6},{6,7},{9,10},{10,11},{13,14},{14,15},{17,18},{18... | collective-permute-start | bytes 884744 | tf_op jit(solution)/shard_map/ppermute | solution.py:125
  23.3 20.6 %collective-permute-start.1 = (bf16[192,768]{1,0:T(8,128)(2,1)S(1)}, bf16[192,768]{1,0:T(8,128)(2,1)S(1)}, u32[]{:S(2)}, u32[]{:S(2)}) collective-permute-start(bf16[192,768]{1,0:T(8,128)(2,1)S(1)} %collective-permute-done), channel_id=1, source_target_pairs={{1,2},{2,3},{5,6},{6,7},{9,10},{10,11},{13,14},{14,15},{17,18},{18... | collective-permute-start | bytes 884744 | tf_op jit(solution)/shard_map/ppermute | solution.py:125
  48.0 84.4 %collective-permute-start.17 = (bf16[768,768]{1,0:T(8,128)(2,1)}, bf16[768,768]{1,0:T(8,128)(2,1)S(1)}, u32[]{:S(2)}, u32[]{:S(2)}) collective-permute-start(bf16[768,768]{1,0:T(8,128)(2,1)} %constant_dynamic-slice_fusion), channel_id=1, source_target_pairs={{0,0},{1,29},{2,30},{3,27},{4,4},{5,1},{6,2},{7,31},{8,8},{9,5},{1... | collective-permute-start | bytes 3538952 | tf_op jit(solution)/shard_map/ppermute | solution.py:191
  52.2 29.8 %collective-permute-start.22 = (bf16[192,768]{1,0:T(8,128)(2,1)S(1)}, bf16[192,768]{1,0:T(8,128)(2,1)S(1)}, u32[]{:S(2)}, u32[]{:S(2)}) collective-permute-start(bf16[192,768]{1,0:T(8,128)(2,1)S(1)} %get-tuple-element.78), channel_id=1, source_target_pairs={{0,2},{1,3},{2,0},{3,1},{4,6},{5,7},{6,4},{7,5},{8,10},{9,11},{10,... | collective-permute-start | bytes 884744 | tf_op jit(solution)/shard_map/ppermute | solution.py:21
  55.0 27.1 %collective-permute-start.23 = (bf16[192,768]{1,0:T(8,128)(2,1)S(1)}, bf16[192,768]{1,0:T(8,128)(2,1)S(1)}, u32[]{:S(2)}, u32[]{:S(2)}) collective-permute-start(bf16[192,768]{1,0:T(8,128)(2,1)S(1)} %get-tuple-element.77), channel_id=1, source_target_pairs={{0,3},{1,0},{2,1},{3,2},{4,7},{5,4},{6,5},{7,6},{8,11},{9,8},{10,9... | collective-permute-start | bytes 884744 | tf_op jit(solution)/shard_map/ppermute | solution.py:21
  58.9 34.5 %collective-permute-start.18 = (bf16[192,768]{1,0:T(8,128)(2,1)S(1)}, bf16[192,768]{1,0:T(8,128)(2,1)S(1)}, u32[]{:S(2)}, u32[]{:S(2)}) collective-permute-start(bf16[192,768]{1,0:T(8,128)(2,1)S(1)} %get-tuple-element.49), channel_id=1, source_target_pairs={{0,1},{1,2},{2,3},{3,0},{4,5},{5,6},{6,7},{7,4},{8,9},{9,10},{10,1... | collective-permute-start | bytes 884744 | tf_op jit(solution)/shard_map/ppermute | solution.py:21
  62.3 40.9 %collective-permute-start.19 = (bf16[192,768]{1,0:T(8,128)(2,1)S(1)}, bf16[192,768]{1,0:T(8,128)(2,1)S(1)}, u32[]{:S(2)}, u32[]{:S(2)}) collective-permute-start(bf16[192,768]{1,0:T(8,128)(2,1)S(1)} %get-tuple-element.50), channel_id=1, source_target_pairs={{0,2},{1,3},{2,0},{3,1},{4,6},{5,7},{6,4},{7,5},{8,10},{9,11},{10,... | collective-permute-start | bytes 884744 | tf_op jit(solution)/shard_map/ppermute | solution.py:21
  82.1 21.2 %collective-permute-start.20 = (bf16[192,768]{1,0:T(8,128)(2,1)S(1)}, bf16[192,768]{1,0:T(8,128)(2,1)S(1)}, u32[]{:S(2)}, u32[]{:S(2)}) collective-permute-start(bf16[192,768]{1,0:T(8,128)(2,1)S(1)} %get-tuple-element.51), channel_id=1, source_target_pairs={{0,3},{1,0},{2,1},{3,2},{4,7},{5,4},{6,5},{7,6},{8,11},{9,8},{10,9... | collective-permute-start | bytes 884744 | tf_op jit(solution)/shard_map/ppermute | solution.py:21
  82.1 24.8 %collective-permute-start.14 = (bf16[192,768]{1,0:T(8,128)(2,1)S(1)}, bf16[192,768]{1,0:T(8,128)(2,1)}, u32[]{:S(2)}, u32[]{:S(2)}) collective-permute-start(bf16[192,768]{1,0:T(8,128)(2,1)S(1)} %get-tuple-element.46), channel_id=1, source_target_pairs={{0,1},{1,2},{2,3},{3,0},{4,5},{5,6},{6,7},{7,4},{8,9},{9,10},{10,1... | collective-permute-start | bytes 884744 | tf_op jit(solution)/shard_map/ppermute | solution.py:21
  93.4 73.2 %collective-permute-start.13 = (bf16[768,768]{1,0:T(8,128)(2,1)}, bf16[768,768]{1,0:T(8,128)(2,1)S(1)}, u32[]{:S(2)}, u32[]{:S(2)}) collective-permute-start(bf16[768,768]{1,0:T(8,128)(2,1)} %constant_dynamic-slice_fusion), channel_id=1, source_target_pairs={{0,28},{1,25},{2,26},{3,23},{4,0},{5,29},{6,30},{7,27},{8,4},{9,1}... | collective-permute-start | bytes 3538952 | tf_op jit(solution)/shard_map/ppermute | solution.py:191
  103.2 19.0 %collective-permute-start.15 = (bf16[192,768]{1,0:T(8,128)(2,1)S(1)}, bf16[192,768]{1,0:T(8,128)(2,1)S(1)}, u32[]{:S(2)}, u32[]{:S(2)}) collective-permute-start(bf16[192,768]{1,0:T(8,128)(2,1)S(1)} %get-tuple-element.47), channel_id=1, source_target_pairs={{0,2},{1,3},{2,0},{3,1},{4,6},{5,7},{6,4},{7,5},{8,10},{9,11},{10,... | collective-permute-start | bytes 884744 | tf_op jit(solution)/shard_map/ppermute | solution.py:21
  103.2 25.8 %collective-permute-start.16 = (bf16[192,768]{1,0:T(8,128)(2,1)S(1)}, bf16[192,768]{1,0:T(8,128)(2,1)S(1)}, u32[]{:S(2)}, u32[]{:S(2)}) collective-permute-start(bf16[192,768]{1,0:T(8,128)(2,1)S(1)} %get-tuple-element.48), channel_id=1, source_target_pairs={{0,3},{1,0},{2,1},{3,2},{4,7},{5,4},{6,5},{7,6},{8,11},{9,8},{10,9... | collective-permute-start | bytes 884744 | tf_op jit(solution)/shard_map/ppermute | solution.py:21
  106.9 91.4 %collective-permute-start.12 = (bf16[768,768]{1,0:T(8,128)(2,1)}, bf16[768,768]{1,0:T(8,128)(2,1)S(1)}, u32[]{:S(2)}, u32[]{:S(2)}) collective-permute-start(bf16[768,768]{1,0:T(8,128)(2,1)} %constant_dynamic-slice_fusion), channel_id=1, source_target_pairs={{0,24},{1,21},{2,22},{3,19},{4,28},{5,25},{6,26},{7,23},{8,0},{9,2... | collective-permute-start | bytes 3538952 | tf_op jit(solution)/shard_map/ppermute | solution.py:191
  122.2 18.2 %collective-permute-start.36 = (bf16[192,768]{1,0:T(8,128)(2,1)}, bf16[192,768]{1,0:T(8,128)(2,1)}, u32[]{:S(2)}, u32[]{:S(2)}) collective-permute-start(bf16[192,768]{1,0:T(8,128)(2,1)} %get-tuple-element.64), channel_id=1, source_target_pairs={{0,1},{1,2},{2,3},{3,0},{4,5},{5,6},{6,7},{7,4},{8,9},{9,10},{10,1... | collective-permute-start | bytes 884744 | tf_op jit(solution)/shard_map/ppermute | solution.py:21
  129.0 23.8 %collective-permute-start.37 = (bf16[192,768]{1,0:T(8,128)(2,1)}, bf16[192,768]{1,0:T(8,128)(2,1)}, u32[]{:S(2)}, u32[]{:S(2)}) collective-permute-start(bf16[192,768]{1,0:T(8,128)(2,1)} %get-tuple-element.65), channel_id=1, source_target_pairs={{0,2},{1,3},{2,0},{3,1},{4,6},{5,7},{6,4},{7,5},{8,10},{9,11},{10,... | collective-permute-start | bytes 884744 | tf_op jit(solution)/shard_map/ppermute | solution.py:21
  132.4 20.4 %collective-permute-start.38 = (bf16[192,768]{1,0:T(8,128)(2,1)}, bf16[192,768]{1,0:T(8,128)(2,1)}, u32[]{:S(2)}, u32[]{:S(2)}) collective-permute-start(bf16[192,768]{1,0:T(8,128)(2,1)} %get-tuple-element.66), channel_id=1, source_target_pairs={{0,3},{1,0},{2,1},{3,2},{4,7},{5,4},{6,5},{7,6},{8,11},{9,8},{10,9... | collective-permute-start | bytes 884744 | tf_op jit(solution)/shard_map/ppermute | solution.py:21
  140.4 46.1 %collective-permute-start.33 = (bf16[192,768]{1,0:T(8,128)(2,1)}, bf16[192,768]{1,0:T(8,128)(2,1)S(1)}, u32[]{:S(2)}, u32[]{:S(2)}) collective-permute-start(bf16[192,768]{1,0:T(8,128)(2,1)} %get-tuple-element.61), channel_id=1, source_target_pairs={{0,1},{1,2},{2,3},{3,0},{4,5},{5,6},{6,7},{7,4},{8,9},{9,10},{10,1... | collective-permute-start | bytes 884744 | tf_op jit(solution)/shard_map/ppermute | solution.py:21
  152.8 36.0 %collective-permute-start.34 = (bf16[192,768]{1,0:T(8,128)(2,1)}, bf16[192,768]{1,0:T(8,128)(2,1)S(1)}, u32[]{:S(2)}, u32[]{:S(2)}) collective-permute-start(bf16[192,768]{1,0:T(8,128)(2,1)} %get-tuple-element.62), channel_id=1, source_target_pairs={{0,2},{1,3},{2,0},{3,1},{4,6},{5,7},{6,4},{7,5},{8,10},{9,11},{10,... | collective-permute-start | bytes 884744 | tf_op jit(solution)/shard_map/ppermute | solution.py:21
  152.8 38.1 %collective-permute-start.35 = (bf16[192,768]{1,0:T(8,128)(2,1)}, bf16[192,768]{1,0:T(8,128)(2,1)}, u32[]{:S(2)}, u32[]{:S(2)}) collective-permute-start(bf16[192,768]{1,0:T(8,128)(2,1)} %get-tuple-element.63), channel_id=1, source_target_pairs={{0,3},{1,0},{2,1},{3,2},{4,7},{5,4},{6,5},{7,6},{8,11},{9,8},{10,9... | collective-permute-start | bytes 884744 | tf_op jit(solution)/shard_map/ppermute | solution.py:21
  166.5 32.5 %collective-permute-start.30 = (bf16[192,768]{1,0:T(8,128)(2,1)S(1)}, bf16[192,768]{1,0:T(8,128)(2,1)S(1)}, u32[]{:S(2)}, u32[]{:S(2)}) collective-permute-start(bf16[192,768]{1,0:T(8,128)(2,1)S(1)} %copy-done.10), channel_id=1, source_target_pairs={{0,1},{1,2},{2,3},{3,0},{4,5},{5,6},{6,7},{7,4},{8,9},{9,10},{10,1... | collective-permute-start | bytes 884744 | tf_op jit(solution)/shard_map/ppermute | solution.py:21
  186.5 23.2 %collective-permute-start.31 = (bf16[192,768]{1,0:T(8,128)(2,1)}, bf16[192,768]{1,0:T(8,128)(2,1)S(1)}, u32[]{:S(2)}, u32[]{:S(2)}) collective-permute-start(bf16[192,768]{1,0:T(8,128)(2,1)} %get-tuple-element.59), channel_id=1, source_target_pairs={{0,2},{1,3},{2,0},{3,1},{4,6},{5,7},{6,4},{7,5},{8,10},{9,11},{10,... | collective-permute-start | bytes 884744 | tf_op jit(solution)/shard_map/ppermute | solution.py:21
  188.8 22.2 %collective-permute-start.32 = (bf16[192,768]{1,0:T(8,128)(2,1)}, bf16[192,768]{1,0:T(8,128)(2,1)S(1)}, u32[]{:S(2)}, u32[]{:S(2)}) collective-permute-start(bf16[192,768]{1,0:T(8,128)(2,1)} %get-tuple-element.60), channel_id=1, source_target_pairs={{0,3},{1,0},{2,1},{3,2},{4,7},{5,4},{6,5},{7,6},{8,11},{9,8},{10,9... | collective-permute-start | bytes 884744 | tf_op jit(solution)/shard_map/ppermute | solution.py:21
  190.9 32.6 %collective-permute-start.27 = (bf16[192,768]{1,0:T(8,128)(2,1)}, bf16[192,768]{1,0:T(8,128)(2,1)S(1)}, u32[]{:S(2)}, u32[]{:S(2)}) collective-permute-start(bf16[192,768]{1,0:T(8,128)(2,1)} %get-tuple-element.55), channel_id=1, source_target_pairs={{0,1},{1,2},{2,3},{3,0},{4,5},{5,6},{6,7},{7,4},{8,9},{9,10},{10,1... | collective-permute-start | bytes 884744 | tf_op jit(solution)/shard_map/ppermute | solution.py:21
  198.3 43.5 %collective-permute-start.28 = (bf16[192,768]{1,0:T(8,128)(2,1)S(1)}, bf16[192,768]{1,0:T(8,128)(2,1)}, u32[]{:S(2)}, u32[]{:S(2)}) collective-permute-start(bf16[192,768]{1,0:T(8,128)(2,1)S(1)} %copy-done.9), channel_id=1, source_target_pairs={{0,2},{1,3},{2,0},{3,1},{4,6},{5,7},{6,4},{7,5},{8,10},{9,11},{10,... | collective-permute-start | bytes 884744 | tf_op jit(solution)/shard_map/ppermute | solution.py:21
  199.0 42.8 %collective-permute-start.29 = (bf16[192,768]{1,0:T(8,128)(2,1)S(1)}, bf16[192,768]{1,0:T(8,128)(2,1)}, u32[]{:S(2)}, u32[]{:S(2)}) collective-permute-start(bf16[192,768]{1,0:T(8,128)(2,1)S(1)} %copy-done.8), channel_id=1, source_target_pairs={{0,3},{1,0},{2,1},{3,2},{4,7},{5,4},{6,5},{7,6},{8,11},{9,8},{10,9... | collective-permute-start | bytes 884744 | tf_op jit(solution)/shard_map/ppermute | solution.py:21
  209.7 39.4 %collective-permute-start.24 = (bf16[192,768]{1,0:T(8,128)(2,1)S(1)}, bf16[192,768]{1,0:T(8,128)(2,1)S(1)}, u32[]{:S(2)}, u32[]{:S(2)}) collective-permute-start(bf16[192,768]{1,0:T(8,128)(2,1)S(1)} %copy-done.7), channel_id=1, source_target_pairs={{0,1},{1,2},{2,3},{3,0},{4,5},{5,6},{6,7},{7,4},{8,9},{9,10},{10,1... | collective-permute-start | bytes 884744 | tf_op jit(solution)/shard_map/ppermute | solution.py:21
  211.0 43.3 %collective-permute-start.25 = (bf16[192,768]{1,0:T(8,128)(2,1)S(1)}, bf16[192,768]{1,0:T(8,128)(2,1)S(1)}, u32[]{:S(2)}, u32[]{:S(2)}) collective-permute-start(bf16[192,768]{1,0:T(8,128)(2,1)S(1)} %copy-done.6), channel_id=1, source_target_pairs={{0,2},{1,3},{2,0},{3,1},{4,6},{5,7},{6,4},{7,5},{8,10},{9,11},{10,... | collective-permute-start | bytes 884744 | tf_op jit(solution)/shard_map/ppermute | solution.py:21
  223.5 30.9 %collective-permute-start.26 = (bf16[192,768]{1,0:T(8,128)(2,1)S(1)}, bf16[192,768]{1,0:T(8,128)(2,1)S(1)}, u32[]{:S(2)}, u32[]{:S(2)}) collective-permute-start(bf16[192,768]{1,0:T(8,128)(2,1)S(1)} %copy-done.5), channel_id=1, source_target_pairs={{0,3},{1,0},{2,1},{3,2},{4,7},{5,4},{6,5},{7,6},{8,11},{9,8},{10,9... | collective-permute-start | bytes 884744 | tf_op jit(solution)/shard_map/ppermute | solution.py:21
  269.1 29.9 %collective-permute-start.41 = (bf16[208,768]{1,0:T(8,128)(2,1)}, bf16[208,768]{1,0:T(8,128)(2,1)S(1)}, u32[]{:S(2)}, u32[]{:S(2)}) collective-permute-start(bf16[208,768]{1,0:T(8,128)(2,1)} %get-tuple-element.69), channel_id=1, source_target_pairs={{0,2},{1,7},{2,4},{3,9},{4,6},{5,11},{6,8},{7,13},{8,10},{9,15},{1... | collective-permute-start | bytes 958472 | tf_op jit(solution)/shard_map/ppermute | solution.py:216
  269.1 30.0 %collective-permute-start.40 = (bf16[208,768]{1,0:T(8,128)(2,1)}, bf16[208,768]{1,0:T(8,128)(2,1)S(1)}, u32[]{:S(2)}, u32[]{:S(2)}) collective-permute-start(bf16[208,768]{1,0:T(8,128)(2,1)} %get-tuple-element.68), channel_id=1, source_target_pairs={{0,1},{1,6},{2,7},{3,8},{4,5},{5,10},{6,11},{7,12},{8,9},{9,14},{1... | collective-permute-start | bytes 958472 | tf_op jit(solution)/shard_map/ppermute | solution.py:216
  269.1 30.1 %collective-permute-start.39 = (bf16[208,768]{1,0:T(8,128)(2,1)}, bf16[208,768]{1,0:T(8,128)(2,1)S(1)}, u32[]{:S(2)}, u32[]{:S(2)}) collective-permute-start(bf16[208,768]{1,0:T(8,128)(2,1)} %get-tuple-element.67), channel_id=1, source_target_pairs={{0,0},{1,5},{2,6},{3,11},{4,4},{5,9},{6,10},{7,15},{8,8},{9,13},{1... | collective-permute-start | bytes 958472 | tf_op jit(solution)/shard_map/ppermute | solution.py:216
  (41 other events, 674.2 us)
